TPU v7x, 128 devices: a whole 4x4x4 slice. The times are simulated.
128 devices in a mesh: sensor: 16 (over y, z_lo, core), channel: 4 (over x), tm: 2 (over z_hi).
Axes of the slice: x: 4, y: 4, z: 4 (z_hi: 2, z_lo: 2; z = z_hi * 2 + z_lo), core: 2. Of those that a mesh axis runs over, the one named last changes fastest.
Arguments:
- tensor: float32 [12288, 128, 512], P('sensor', 'tm', 'channel'), may hold values from -6 to 6
- core: float32 [64, 64, 32], replicated, may hold values from -0.015625 to 0.015625
- sensor_factor: float32 [12288, 64], P('sensor'), may hold values from -6 to 6
- channel_factor: float32 [512, 64], P('channel'), may hold values from -6 to 6
- time_factor: float32 [128, 32], P('tm'), may hold values from -6 to 6
- neighbour_ids: int32 [96, 4], P('sensor'), may hold values from 0 to 95
- edge_weights: int32 [96, 4, 128, 128], P('sensor'), may hold values from 0 to 3
Outputs:
- core_grad: float32 [64, 64, 32], replicated
- sensor_grad: float32 [12288, 64], P(('sensor', 'channel', 'tm'))
- channel_grad: float32 [512, 64], P('channel')
- time_grad: float32 [128, 32], P('tm')
All inputs are finite; a program needn't handle non-finite values.
Results may differ from a plain program's by a relative error of at most 0.0001.
Values sent between devices are 32-bit elements; how exact they have to be, the bound alone decides.
A program may use at most 192 MiB of HBM per device.

v0:
```python
import math
import jax
import jax.numpy as jnp
from jax import lax
from jax.sharding import PartitionSpec as P

lap_weight = 1.0 / 512.0
highest = lax.Precision.HIGHEST


def pulled_rows(whole_factor, neighbour_ids, weights_float, block):
    whole = whole_factor.reshape(-1, block, whole_factor.shape[-1])
    neighbours = whole[neighbour_ids]
    return jnp.einsum("bnic,bncd->bid", weights_float, neighbours, precision=highest)


def on_device(
    tensor, core, sensor_factor, channel_factor, time_factor, neighbour_ids, edge_weights
):
    sensor_rows, time_rows, chan_rows = tensor.shape
    rank_one, rank_two, rank_three = core.shape
    n_sensor = lax.axis_size("sensor")
    n_channel = lax.axis_size("channel")
    n_time = lax.axis_size("tm")
    total_sensors = sensor_rows * n_sensor
    total_time = time_rows * n_time
    total_chan = chan_rows * n_channel
    core_time = jnp.einsum("rst,kt->rks", core, time_factor, precision=highest)
    core_both = jnp.einsum("rks,js->rkj", core_time, channel_factor, precision=highest)
    core_chan = jnp.einsum("rst,js->rtj", core, channel_factor, precision=highest)
    flat_core = core_both.reshape(rank_one, time_rows * chan_rows)
    residual = jnp.dot(sensor_factor, flat_core, precision=highest) - tensor.reshape(
        sensor_rows, time_rows * chan_rows
    )
    folded = jnp.dot(sensor_factor.T, residual, precision=highest)
    fit_part = jnp.dot(residual, flat_core.T, precision=highest) / math.sqrt(
        total_time * total_chan
    )
    folded3 = folded.reshape(rank_one, time_rows, chan_rows)
    inner = jnp.einsum("rkj,js->rks", folded3, channel_factor, precision=highest)
    core_part = jnp.einsum("rks,kt->rst", inner, time_factor, precision=highest) / math.sqrt(
        total_sensors * total_time * total_chan
    )
    chan_part = jnp.einsum("rkj,rks->js", folded3, core_time, precision=highest) / math.sqrt(
        total_sensors * total_time
    )
    time_part = jnp.einsum("rkj,rtj->kt", folded3, core_chan, precision=highest) / math.sqrt(
        total_sensors * total_chan
    )
    groups = n_channel * n_time
    share_index = lax.axis_index("channel") * n_time + lax.axis_index("tm")
    share = sensor_rows // groups
    block = edge_weights.shape[-1]
    weights_float = edge_weights.astype(jnp.float32)
    degree = jnp.sum(weights_float, axis=(1, 3)).reshape(sensor_rows)
    reduced = lax.psum_scatter(fit_part, ("channel", "tm"), scatter_dimension=0, tiled=True)
    whole_rows = lax.all_gather(sensor_factor, "sensor", axis=0, tiled=True)
    pulled = pulled_rows(whole_rows, neighbour_ids, weights_float, block).reshape(
        sensor_rows, rank_one
    )
    graph_all = lap_weight * (degree[:, None] * sensor_factor - pulled)
    graph_share = lax.dynamic_slice_in_dim(graph_all, share_index * share, share, 0)
    sensor_grad = reduced + graph_share
    core_grad = lax.psum(core_part, ("sensor", "channel", "tm"))
    channel_grad = lax.psum(chan_part, ("sensor", "tm"))
    time_grad = lax.psum(time_part, ("sensor", "channel"))
    return (core_grad, sensor_grad, channel_grad, time_grad)


def solution(mesh):
    return jax.shard_map(
        on_device,
        mesh=mesh,
        in_specs=(
            P("sensor", "tm", "channel"),
            P(),
            P("sensor", None),
            P("channel", None),
            P("tm", None),
            P("sensor", None),
            P("sensor", None, None, None),
        ),
        out_specs=(P(), P(("sensor", "channel", "tm"), None), P("channel", None), P("tm", None)),
        check_vma=False,
    )
```

profile of v0, /device:TPU:0, one launch (start us, length us, event | category | flops | bytes accessed | tf_op | source)
XLA Modules:
  0.0 556.5 jit_solution(13374377818562630704)
XLA Ops:
  8.1 24.9 %copy.27 = f32[768,64,128]{0,2,1:T(8,128)} copy(f32[768,64,128]{2,1,0:T(8,128)} %param.7) | data formatting | bytes 50331648 | tf_op args[0]
  33.0 1.8 fusion.32
  34.8 1.8 fusion.5
  36.7 26.3 %bitcast_subtract_fusion = f32[768,8192]{0,1:T(8,128)} fusion(f32[768,64,128]{0,2,1:T(8,128)} %copy.27, f32[768,64]{0,1:T(8,128)S(1)} %copy-done.3, f32[8,8,64,128]{3,2,1,0:T(8,128)S(1)} %bitcast.77), kind=kOutput, calls=%fused_computation.1 | convolution fusion | flops 4838129664 | bytes 52625408 | tf_op jit(solution)/shard_map/dot_general | solution.py:32
  63.0 20.9 %fusion.14 = f32[768,64]{0,1:T(8,128)S(1)} fusion(f32[768,8192]{0,1:T(8,128)} %bitcast_subtract_fusion, f32[8,8,64,128]{3,2,1,0:T(8,128)S(1)} %bitcast.78), kind=kOutput, calls=%fused_computation.18 | convolution fusion | flops 4831887360 | bytes 27459584 | tf_op jit(solution)/shard_map/dot_general | solution.py:36
  83.8 0.9 copy.34
  84.8 0.5 all-gather.2.cloned.1.call-update
  85.4 27.7 %convolution_bitcast_fusion = f32[8,8,64,128]{3,1,2,0:T(8,128)S(1)} fusion(f32[768,8192]{0,1:T(8,128)} %bitcast_subtract_fusion, f32[768,64]{0,1:T(8,128)S(1)} %copy-done.4), kind=kOutput, calls=%fused_computation.12 | convolution fusion | flops 4831838208 | bytes 27459584 | tf_op jit(solution)/shard_map/dot_general | solution.py:35
  113.1 0.4 copy.39
  113.5 1.9 fusion.28
  115.4 2.2 convolution_multiply_fusion
  117.6 5.2 fusion.20
  122.9 1.9 fusion.26
  124.8 0.1 copy.28
  125.0 1.6 convert_reduce_fusion
  126.6 129.7 %psum.22 = f32[128,64]{0,1:T(8,128)} all-reduce(f32[128,64]{0,1:T(8,128)S(1)} %fusion.20), channel_id=1, replica_groups=mesh['sensor'=16,'channel'=4,'tm'=2] {'sensor','tm'}, use_global_device_ids=true, to_apply=%region_3.0 | all-reduce | flops 8192 | bytes 65536 | tf_op jit(solution)/shard_map/psum | solution.py:65
  256.3 3.0 fusion.23
  259.3 276.5 %psum.23 = f32[64,32]{0,1:T(8,128)} all-reduce(f32[64,32]{0,1:T(8,128)S(1)} %fusion.23), channel_id=1, replica_groups=mesh['sensor'=16,'channel'=4,'tm'=2] {'sensor','channel'}, use_global_device_ids=true, to_apply=%region_4.0 | all-reduce | flops 2048 | bytes 16384 | tf_op jit(solution)/shard_map/psum | solution.py:66
  535.9 0.9 copy.35
  536.8 4.0 copy_bitcast_fusion
  540.8 2.6 gather_fusion
  543.4 1.8 fusion.11
  545.2 1.6 fusion.25
  546.8 2.3 copy.54
  (29 shorter events, 0.4 us)
Async XLA Ops:
  8.0 25.0 %copy-start = (f32[64,64,32]{1,2,0:T(8,128)S(1)}, f32[64,64,32]{1,2,0:T(8,128)}, u32[]{:S(2)}) copy-start(f32[64,64,32]{1,2,0:T(8,128)} %param.8) | copy-start | bytes 1572868
  8.0 24.9 %copy-start.6 = (f32[64,32]{0,1:T(8,128)S(1)}, f32[64,32]{0,1:T(8,128)}, u32[]{:S(2)}) copy-start(f32[64,32]{0,1:T(8,128)} %param.11) | copy-start | bytes 24580
  8.0 527.9 %reduce-scatter.4.cloned.1.call-start = ((), (), s32[]{:S(2)}) async-start(), calls=%async_computation.3 | async-start | bytes 442368
  33.0 1.8 copy-start.5
  34.8 1.9 copy-start.1
  34.8 1.9 copy-start.3
  63.0 22.5 %copy-start.4 = (f32[768,64]{0,1:T(8,128)S(1)}, f32[768,64]{0,1:T(8,128)}, u32[]{:S(2)}) copy-start(f32[768,64]{0,1:T(8,128)} %param.9) | copy-start | bytes 589828
  84.8 452.0 %all-gather.2.cloned.1.call-start = ((), (), s32[]{:S(2)}) async-start(), calls=%async_computation.2 | async-start | bytes 3342336 | tf_op jit(solution)/shard_map/all_gather | solution.py:57
  85.4 461.4 %all-reduce.2.cloned.1.call-start = ((), (), s32[]{:S(2)}) async-start(), calls=%async_computation.1 | async-start | bytes 2097152 | tf_op jit(solution)/shard_map/psum | solution.py:64
  122.9 1.9 copy-start.7
  540.8 2.6 copy-start.2
Sparse Core Ops, SparseCore 0:
  84.9 73.7 reduce-scatter.3
  164.1 146.2 all-reduce.1
Sparse Core Ops, SparseCore 1:
  87.0 38.2 all-gather.1
where the time goes:
time: 557 us; the launch traced here: 556 us
  blocking collectives  406 us (73%)
  matrix products  94.5 us (17%)
  local copies, waits for them, and re-layouts  36.2 us (6%)
  between operations  15.7 us (3%)
    psum x1, blocking collectives, on_device(): time_grad = lax.psum(time_part, ('sensor', 'channel'))  277 us
    psum x1, blocking collectives, on_device(): channel_grad = lax.psum(chan_part, ('sensor', 'tm'))  130 us
    unnamed x21, local copies, waits for them, and re-layouts  29.4 us
    dot_general x1, matrix products, on_device(): folded = jnp.dot(sensor_factor.T, residual, precision=highest)  27.7 us
    dot_general x1, matrix products, on_device(): jnp.dot(sensor_factor, flat_core, precision=highest)  26.3 us
    dot_general x1, matrix products, on_device(): jnp.dot(residual, flat_core.T, precision=highest)  20.9 us
  transfers between devices with their start and end apart: 3, of which 0 were waited for; matrix products, arithmetic and copies ran while one was open for 10% of the time, Pallas kernels for 0%

commit v1 on v0

--- a/solution.py
+++ b/solution.py
@@ -63,7 +63,7 @@
     sensor_grad = reduced + graph_share
     core_grad = lax.psum(core_part, ("sensor", "channel", "tm"))
     channel_grad = lax.psum(chan_part, ("sensor", "tm"))
-    time_grad = lax.psum(time_part, ("sensor", "channel"))
+    time_grad = jnp.sum(lax.all_gather(time_part, ("sensor", "channel")), axis=0)
     return (core_grad, sensor_grad, channel_grad, time_grad)
 
 

time: 557 us -> 425 us (0.76)
  blocking collectives: 406 us -> 273 us
    psum x1 -> x0, blocking collectives: 277 us -> none  [on_device(): time_grad = lax.psum(time_part, ('sensor', 'channel'))]
    all_gather x0 -> x1, blocking collectives: none -> 143 us  [on_device(): lax.all_gather(time_part, ('sensor', 'channel'))]
  transfers between devices with their start and end apart: 3 -> 3, of which waited for: 0 -> 0; matrix products, arithmetic and copies ran while one was open for 10% -> 13% of each run, Pallas kernels for 0% -> 0%
where the time goes in v1:
time: 425 us; the launch traced here: 424 us
  blocking collectives  273 us (64%)
  matrix products  94.5 us (22%)
  local copies, waits for them, and re-layouts  36.2 us (9%)
  between operations  15.7 us (4%)
    all_gather x1, blocking collectives, on_device(): lax.all_gather(time_part, ('sensor', 'channel'))  143 us
    psum x1, blocking collectives, on_device(): channel_grad = lax.psum(chan_part, ('sensor', 'tm'))  130 us
    unnamed x21, local copies, waits for them, and re-layouts  29.4 us
    dot_general x1, matrix products, on_device(): folded = jnp.dot(sensor_factor.T, residual, precision=highest)  27.7 us
    dot_general x1, matrix products, on_device(): jnp.dot(sensor_factor, flat_core, precision=highest)  26.3 us
    dot_general x1, matrix products, on_device(): jnp.dot(residual, flat_core.T, precision=highest)  20.9 us
  transfers between devices with their start and end apart: 3, of which 0 were waited for; matrix products, arithmetic and copies ran while one was open for 13% of the time, Pallas kernels for 0%

profile of v1, /device:TPU:0, one launch (start us, length us, event | category | flops | bytes accessed | tf_op | source)
XLA Modules:
  0.0 423.7 jit_solution(4798195538514744745)
XLA Ops:
  8.1 24.9 %copy.27 = f32[768,64,128]{0,2,1:T(8,128)} copy(f32[768,64,128]{2,1,0:T(8,128)} %param.7) | data formatting | bytes 50331648 | tf_op args[0]
  33.0 1.8 fusion.33
  34.8 1.8 fusion.5
  36.7 26.3 %bitcast_subtract_fusion = f32[768,8192]{0,1:T(8,128)} fusion(f32[768,64,128]{0,2,1:T(8,128)} %copy.27, f32[768,64]{0,1:T(8,128)S(1)} %copy-done.3, f32[8,8,64,128]{3,2,1,0:T(8,128)S(1)} %bitcast.81), kind=kOutput, calls=%fused_computation.1 | convolution fusion | flops 4838129664 | bytes 52625408 | tf_op jit(solution)/shard_map/dot_general | solution.py:32
  63.0 20.9 %fusion.14 = f32[768,64]{0,1:T(8,128)S(1)} fusion(f32[768,8192]{0,1:T(8,128)} %bitcast_subtract_fusion, f32[8,8,64,128]{3,2,1,0:T(8,128)S(1)} %bitcast.82), kind=kOutput, calls=%fused_computation.18 | convolution fusion | flops 4831887360 | bytes 27459584 | tf_op jit(solution)/shard_map/dot_general | solution.py:36
  83.8 0.9 copy.34
  84.8 0.5 all-gather.4.cloned.1.call-update
  85.4 27.7 %convolution_bitcast_fusion = f32[8,8,64,128]{3,1,2,0:T(8,128)S(1)} fusion(f32[768,8192]{0,1:T(8,128)} %bitcast_subtract_fusion, f32[768,64]{0,1:T(8,128)S(1)} %copy-done.4), kind=kOutput, calls=%fused_computation.12 | convolution fusion | flops 4831838208 | bytes 27459584 | tf_op jit(solution)/shard_map/dot_general | solution.py:35
  113.1 0.4 copy.39
  113.5 1.9 fusion.29
  115.4 2.2 convolution_multiply_fusion
  117.6 5.2 %fusion.20 = f32[128,64]{0,1:T(8,128)S(1)} fusion(f32[64,64,128]{2,1,0:T(8,128)S(1)} %bitcast.79, f32[64,64,64]{2,0,1:T(8,128)} %copy-done.1), kind=kOutput, calls=%fused_computation.20 | convolution fusion | flops 402661376 | bytes 3178496 | tf_op jit(solution)/shard_map/rkj,rks->js/dot_general | solution.py:44
  122.9 1.9 fusion.27
  125.0 1.6 convert_reduce_fusion
  126.6 129.7 %psum.15 = f32[128,64]{0,1:T(8,128)} all-reduce(f32[128,64]{0,1:T(8,128)S(1)} %fusion.20), channel_id=1, replica_groups=mesh['sensor'=16,'channel'=4,'tm'=2] {'sensor','tm'}, use_global_device_ids=true, to_apply=%region_3.0 | all-reduce | flops 8192 | bytes 65536 | tf_op jit(solution)/shard_map/psum | solution.py:65
  256.3 3.0 fusion.24
  259.3 143.1 %all-gather.1 = f32[64,64,32]{1,2,0:T(8,128)S(1)} all-gather(f32[1,64,32]{1,2,0:T(8,128)S(1)} %fusion.24), channel_id=2, replica_groups=mesh['sensor'=16,'channel'=4,'tm'=2] {'sensor','channel'}, dimensions={0}, use_global_device_ids=true | all-gather | bytes 532480 | tf_op jit(solution)/shard_map/all_gather | solution.py:66
  402.5 0.7 reduce_sum.19
  403.2 0.9 copy.35
  404.1 4.0 copy_bitcast_fusion
  408.0 2.6 gather_fusion
  410.7 1.8 fusion.11
  412.5 1.6 fusion.26
  414.0 2.3 copy.54
  (30 shorter events, 0.5 us)
Async XLA Ops:
  8.0 25.0 %copy-start = (f32[64,64,32]{1,2,0:T(8,128)S(1)}, f32[64,64,32]{1,2,0:T(8,128)}, u32[]{:S(2)}) copy-start(f32[64,64,32]{1,2,0:T(8,128)} %param.8) | copy-start | bytes 1572868
  8.0 24.9 %copy-start.6 = (f32[64,32]{0,1:T(8,128)S(1)}, f32[64,32]{0,1:T(8,128)}, u32[]{:S(2)}) copy-start(f32[64,32]{0,1:T(8,128)} %param.11) | copy-start | bytes 24580
  8.0 395.1 %reduce-scatter.4.cloned.1.call-start = ((), (), s32[]{:S(2)}) async-start(), calls=%async_computation.3 | async-start | bytes 442368
  33.0 1.8 copy-start.5
  34.8 1.9 copy-start.1
  34.8 1.9 copy-start.3
  63.0 22.5 %copy-start.4 = (f32[768,64]{0,1:T(8,128)S(1)}, f32[768,64]{0,1:T(8,128)}, u32[]{:S(2)}) copy-start(f32[768,64]{0,1:T(8,128)} %param.9) | copy-start | bytes 589828
  84.8 319.3 %all-gather.4.cloned.1.call-start = ((), (), s32[]{:S(2)}) async-start(), calls=%async_computation.2 | async-start | bytes 3342336 | tf_op jit(solution)/shard_map/all_gather | solution.py:57
  85.4 328.7 %all-reduce.2.cloned.1.call-start = ((), (), s32[]{:S(2)}) async-start(), calls=%async_computation.1 | async-start | bytes 2097152 | tf_op jit(solution)/shard_map/psum | solution.py:64
  122.9 1.9 copy-start.7
  408.0 2.6 copy-start.2
Sparse Core Ops, SparseCore 0:
  84.9 73.7 reduce-scatter.3
  164.1 146.2 all-reduce.1
Sparse Core Ops, SparseCore 1:
  87.0 38.2 all-gather.3

commit v2 on v0

--- a/solution.py
+++ b/solution.py
@@ -63,7 +63,7 @@
     sensor_grad = reduced + graph_share
     core_grad = lax.psum(core_part, ("sensor", "channel", "tm"))
     channel_grad = lax.psum(chan_part, ("sensor", "tm"))
-    time_grad = lax.psum(time_part, ("sensor", "channel"))
+    time_grad = lax.psum(lax.psum(time_part, "sensor"), "channel")
     return (core_grad, sensor_grad, channel_grad, time_grad)
 
 

time: 557 us -> 351 us (0.63)
  blocking collectives: 406 us -> 200 us
    psum x1 -> x2, blocking collectives: 277 us -> 70.4 us  [on_device(): time_grad = lax.psum(lax.psum(time_part, 'sensor'), 'channel')]
  transfers between devices with their start and end apart: 3 -> 3, of which waited for: 0 -> 0; matrix products, arithmetic and copies ran while one was open for 10% -> 16% of each run, Pallas kernels for 0% -> 0%
where the time goes in v2:
time: 351 us; the launch traced here: 350 us
  blocking collectives  200 us (57%)
  matrix products  94.5 us (27%)
  local copies, waits for them, and re-layouts  36.2 us (10%)
  between operations  15.7 us (4%)
    psum x1, blocking collectives, on_device(): channel_grad = lax.psum(chan_part, ('sensor', 'tm'))  130 us
    psum x2, blocking collectives, on_device(): time_grad = lax.psum(lax.psum(time_part, 'sensor'), 'channel')  70.4 us
    unnamed x21, local copies, waits for them, and re-layouts  29.3 us
    dot_general x1, matrix products, on_device(): folded = jnp.dot(sensor_factor.T, residual, precision=highest)  27.7 us
    dot_general x1, matrix products, on_device(): jnp.dot(sensor_factor, flat_core, precision=highest)  26.3 us
    dot_general x1, matrix products, on_device(): jnp.dot(residual, flat_core.T, precision=highest)  20.9 us
  transfers between devices with their start and end apart: 3, of which 0 were waited for; matrix products, arithmetic and copies ran while one was open for 16% of the time, Pallas kernels for 0%

profile of v2, /device:TPU:0, one launch (start us, length us, event | category | flops | bytes accessed | tf_op | source)
XLA Modules:
  0.0 350.4 jit_solution(4612580875231637469)
XLA Ops:
  8.1 24.9 %copy.27 = f32[768,64,128]{0,2,1:T(8,128)} copy(f32[768,64,128]{2,1,0:T(8,128)} %param.7) | data formatting | bytes 50331648 | tf_op args[0]
  33.0 1.8 fusion.32
  34.8 1.8 fusion.5
  36.7 26.3 %bitcast_subtract_fusion = f32[768,8192]{0,1:T(8,128)} fusion(f32[768,64,128]{0,2,1:T(8,128)} %copy.27, f32[768,64]{0,1:T(8,128)S(1)} %copy-done.3, f32[8,8,64,128]{3,2,1,0:T(8,128)S(1)} %bitcast.77), kind=kOutput, calls=%fused_computation.1 | convolution fusion | flops 4838129664 | bytes 52625408 | tf_op jit(solution)/shard_map/dot_general | solution.py:32
  63.0 20.9 %fusion.14 = f32[768,64]{0,1:T(8,128)S(1)} fusion(f32[768,8192]{0,1:T(8,128)} %bitcast_subtract_fusion, f32[8,8,64,128]{3,2,1,0:T(8,128)S(1)} %bitcast.78), kind=kOutput, calls=%fused_computation.18 | convolution fusion | flops 4831887360 | bytes 27459584 | tf_op jit(solution)/shard_map/dot_general | solution.py:36
  83.8 0.9 copy.34
  84.8 0.5 all-gather.2.cloned.1.call-update
  85.4 27.7 %convolution_bitcast_fusion = f32[8,8,64,128]{3,1,2,0:T(8,128)S(1)} fusion(f32[768,8192]{0,1:T(8,128)} %bitcast_subtract_fusion, f32[768,64]{0,1:T(8,128)S(1)} %copy-done.4), kind=kOutput, calls=%fused_computation.12 | convolution fusion | flops 4831838208 | bytes 27459584 | tf_op jit(solution)/shard_map/dot_general | solution.py:35
  113.1 0.4 copy.39
  113.5 1.9 fusion.28
  115.4 2.2 convolution_multiply_fusion
  117.6 5.2 %fusion.20 = f32[128,64]{0,1:T(8,128)S(1)} fusion(f32[64,64,128]{2,1,0:T(8,128)S(1)} %bitcast.75, f32[64,64,64]{2,0,1:T(8,128)} %copy-done.1), kind=kOutput, calls=%fused_computation.20 | convolution fusion | flops 402661376 | bytes 3178496 | tf_op jit(solution)/shard_map/rkj,rks->js/dot_general | solution.py:44
  122.9 2.0 fusion.26
  125.0 1.6 convert_reduce_fusion
  126.6 129.7 %psum.29 = f32[128,64]{0,1:T(8,128)} all-reduce(f32[128,64]{0,1:T(8,128)S(1)} %fusion.20), channel_id=1, replica_groups=mesh['sensor'=16,'channel'=4,'tm'=2] {'sensor','tm'}, use_global_device_ids=true, to_apply=%region_3.0 | all-reduce | flops 8192 | bytes 65536 | tf_op jit(solution)/shard_map/psum | solution.py:65
  256.3 3.0 fusion.23
  259.3 52.9 %psum.30 = f32[64,32]{0,1:T(8,128)S(1)} all-reduce(f32[64,32]{0,1:T(8,128)S(1)} %fusion.23), channel_id=1, replica_groups=mesh['sensor'=16,'channel'=4,'tm'=2] {'sensor'}, use_global_device_ids=true, to_apply=%region_4.0 | all-reduce | flops 2048 | bytes 16384 | tf_op jit(solution)/shard_map/psum | solution.py:66
  312.2 17.5 %psum.31 = f32[64,32]{0,1:T(8,128)} all-reduce(f32[64,32]{0,1:T(8,128)S(1)} %psum.30), channel_id=1, replica_groups=mesh['sensor'=16,'channel'=4,'tm'=2] {'channel'}, use_global_device_ids=true, to_apply=%region_5.0 | all-reduce | flops 2048 | bytes 16384 | tf_op jit(solution)/shard_map/psum | solution.py:66
  329.8 0.9 copy.35
  330.7 4.0 %copy_bitcast_fusion = f32[96,128,64]{1,2,0:T(8,128)} fusion(f32[12288,64]{0,1:T(8,128)} %all-gather.2.cloned.1.call-done), kind=kLoop, calls=%fused_computation.2 | loop fusion | bytes 6291456 | tf_op jit(solution)/shard_map/reshape | solution.py:12
  334.7 2.6 gather_fusion
  337.3 1.8 fusion.11
  339.1 1.6 fusion.25
  340.7 2.3 copy.54
  (30 shorter events, 0.5 us)
Async XLA Ops:
  8.0 24.9 %copy-start = (f32[64,64,32]{1,2,0:T(8,128)S(1)}, f32[64,64,32]{1,2,0:T(8,128)}, u32[]{:S(2)}) copy-start(f32[64,64,32]{1,2,0:T(8,128)} %param.8) | copy-start | bytes 1572868
  8.0 24.9 %copy-start.6 = (f32[64,32]{0,1:T(8,128)S(1)}, f32[64,32]{0,1:T(8,128)}, u32[]{:S(2)}) copy-start(f32[64,32]{0,1:T(8,128)} %param.11) | copy-start | bytes 24580
  8.0 321.8 %reduce-scatter.4.cloned.1.call-start = ((), (), s32[]{:S(2)}) async-start(), calls=%async_computation.3 | async-start | bytes 442368
  32.9 1.9 copy-start.5
  34.8 1.9 copy-start.1
  34.8 1.9 copy-start.3
  63.0 22.5 %copy-start.4 = (f32[768,64]{0,1:T(8,128)S(1)}, f32[768,64]{0,1:T(8,128)}, u32[]{:S(2)}) copy-start(f32[768,64]{0,1:T(8,128)} %param.9) | copy-start | bytes 589828
  84.8 245.9 %all-gather.2.cloned.1.call-start = ((), (), s32[]{:S(2)}) async-start(), calls=%async_computation.2 | async-start | bytes 3342336 | tf_op jit(solution)/shard_map/all_gather | solution.py:57
  85.4 255.3 %all-reduce.2.cloned.1.call-start = ((), (), s32[]{:S(2)}) async-start(), calls=%async_computation.1 | async-start | bytes 2097152 | tf_op jit(solution)/shard_map/psum | solution.py:64
  122.8 2.0 copy-start.7
  334.7 2.6 copy-start.2
Sparse Core Ops, SparseCore 0:
  84.9 73.8 reduce-scatter.3
  164.1 146.0 all-reduce.1
Sparse Core Ops, SparseCore 1:
  87.0 38.2 all-gather.1
